TPU v7x, 32 devices: a whole 2x2x4 slice. The times are simulated.
32 devices in a mesh: ep: 8 (over z, x), tp: 4 (over y, core).
Axes of the slice: x: 2, y: 2, z: 4, core: 2. Of those that a mesh axis runs over, the one named last changes fastest.
Arguments:
- hidden_in: bfloat16 [1024, 2048], P('ep', 'tp'), may hold values from -6 to 6
- norm_gain: float32 [2048], replicated, may hold values from 0.5 to 1.5
- router_weight: bfloat16 [2048, 8], replicated, may hold values from -4.861359 to 4.861359
- shared_gate_up: bfloat16 [2048, 2, 1408], P(None, None, 'tp'), may hold values from -0.125 to 0.125
- shared_down: bfloat16 [1408, 2048], P('tp'), may hold values from -0.15625 to 0.15625
- slot_gate_up: bfloat16 [32, 2048, 2, 704], P(('ep', 'tp')), as said below
- slot_down: bfloat16 [32, 704, 2048], P(('ep', 'tp')), as said below
- slot_expert: int32 [32], replicated, may hold values from 0 to 7, as said below
- slot_choice: int32 [1024, 6], P('ep'), may hold values from 0 to 31, all different within a row; in each aligned block of 32 rows (0 to 31, 32 to 63, ...) at most 12 rows name the same one
- live_count: int32 [8], P('ep'), may hold values from 64 to 128, as said below
Outputs:
- mixed_out: bfloat16 [1024, 2048], P('ep', 'tp')
Inputs may be any that keep to these rules, and one draw needn't show every extreme that they name: `slot_expert`: each expert is held by 1 or 7 slots; exactly 4 experts by the larger number. `slot_gate_up`: entry s holds the weights of expert slot_expert[s]; slots of one expert hold equal weights. `slot_down`: entry s holds the weights of expert slot_expert[s]; slots of one expert hold equal weights. `slot_choice`: a row names 6 different slots; in each aligned block of 32 rows no slot is named more than 12 times. `live_count`: the live rows of an index of ep are its first ones; some index of ep has all 128 rows live.
All inputs are finite; a program needn't handle non-finite values.
Results may differ from a plain program's by a relative error of at most 0.0058.
Values may be sent and summed in bfloat16 or wider, within the bound.
A program may use at most 64 MiB of HBM per device.

v0:
```python
import jax
import jax.numpy as jnp
from jax import lax
from jax.sharding import PartitionSpec as P


def gate_weights(normed_rows, choices, router_weight, slot_expert):
    logits = jnp.dot(normed_rows, router_weight, preferred_element_type=jnp.float32)
    slot_total = slot_expert.shape[0]
    expert_total = router_weight.shape[1]
    slot_hit = choices[:, :, None] == jnp.arange(slot_total, dtype=jnp.int32)
    expert_ids = jnp.sum(jnp.where(slot_hit, slot_expert, 0), axis=2)
    expert_hit = expert_ids[:, :, None] == jnp.arange(expert_total, dtype=jnp.int32)
    picked = jnp.sum(jnp.where(expert_hit, logits[:, None, :], 0.0), axis=2)
    highest = jnp.max(picked, axis=1, keepdims=True)
    weights = jnp.exp(picked - highest)
    return (weights / jnp.sum(weights, axis=1, keepdims=True)).astype(jnp.bfloat16)


def slot_positions(targets):
    length = targets.shape[0]
    same_slot = targets[:, None] == targets[None, :]
    earlier = jnp.arange(length)[None, :] < jnp.arange(length)[:, None]
    return jnp.sum(same_slot & earlier, axis=1)


def expert_apply(received, slot_gate_up, slot_down):
    shape_in = received.shape
    flat_rows = received.reshape(-1, shape_in[-1])
    gate_up = jnp.einsum(
        "rd,dgf->rgf", flat_rows, slot_gate_up[0], preferred_element_type=jnp.float32
    )
    activated = (jax.nn.silu(gate_up[:, 0]) * gate_up[:, 1]).astype(jnp.bfloat16)
    result = jnp.dot(activated, slot_down[0], preferred_element_type=jnp.float32).astype(
        jnp.bfloat16
    )
    return result.reshape(shape_in)


def local(
    hidden_in,
    norm_gain,
    router_weight,
    shared_gate_up,
    shared_down,
    slot_gate_up,
    slot_down,
    slot_expert,
    slot_choice,
    live_count,
):
    tp_count = lax.axis_size("tp")
    ep_count = lax.axis_size("ep")
    tp_index = lax.axis_index("tp")
    tok_count = hidden_in.shape[0]
    feature_width = hidden_in.shape[1] * tp_count
    top_count = slot_choice.shape[1]
    slot_count = slot_expert.shape[0]
    quarter = tok_count // tp_count
    capacity = max(2, 2 * quarter * top_count // slot_count)
    full_rows = lax.all_gather(hidden_in, "tp", axis=1, tiled=True)
    wide_rows = full_rows.astype(jnp.float32)
    norm_scale = lax.rsqrt(jnp.mean(wide_rows * wide_rows, axis=1, keepdims=True) + 1e-06)
    normed = (wide_rows * norm_scale * norm_gain).astype(jnp.bfloat16)
    shared_proj = jnp.einsum(
        "td,dgf->tgf", normed, shared_gate_up, preferred_element_type=jnp.float32
    )
    shared_hidden = (jax.nn.silu(shared_proj[:, 0]) * shared_proj[:, 1]).astype(jnp.bfloat16)
    partial_value = jnp.dot(shared_hidden, shared_down, preferred_element_type=jnp.float32)
    row_start = tp_index * quarter
    own_rows = lax.dynamic_slice_in_dim(normed, row_start, quarter, 0)
    own_choice = lax.dynamic_slice_in_dim(slot_choice, row_start, quarter, 0)
    gate_values = gate_weights(own_rows, own_choice, router_weight, slot_expert)
    targets = own_choice.reshape(-1)
    placed = targets * capacity + slot_positions(targets)
    outgoing = jnp.zeros((slot_count * capacity, feature_width), jnp.bfloat16)
    outgoing = outgoing.at[placed].set(jnp.repeat(own_rows, top_count, axis=0))
    outgoing = outgoing.reshape(ep_count, tp_count, capacity, feature_width)
    arrived = lax.all_to_all(
        lax.all_to_all(outgoing, "ep", split_axis=0, concat_axis=0, tiled=True),
        "tp",
        split_axis=1,
        concat_axis=1,
        tiled=True,
    )
    computed = expert_apply(arrived, slot_gate_up, slot_down)
    returned = lax.all_to_all(
        lax.all_to_all(computed, "ep", split_axis=0, concat_axis=0, tiled=True),
        "tp",
        split_axis=1,
        concat_axis=1,
        tiled=True,
    )
    fetched = returned.reshape(-1, feature_width)[placed].reshape(quarter, top_count, feature_width)
    routed = jnp.einsum("qk,qkd->qd", gate_values, fetched, preferred_element_type=jnp.float32)
    own_partial = lax.dynamic_slice_in_dim(partial_value, row_start, quarter, 0) + routed
    partial_value = lax.dynamic_update_slice_in_dim(partial_value, own_partial, row_start, 0)
    summed = lax.psum_scatter(partial_value, "tp", scatter_dimension=1, tiled=True)
    live_rows = jnp.arange(tok_count, dtype=jnp.int32) < live_count[0]
    mixed_out = jnp.where(live_rows[:, None], hidden_in.astype(jnp.float32) + summed, 0.0)
    return mixed_out.astype(jnp.bfloat16)


def solution(mesh):
    in_specs = (
        P("ep", "tp"),
        P(),
        P(),
        P(None, None, "tp"),
        P("tp", None),
        P(("ep", "tp"), None, None, None),
        P(("ep", "tp"), None, None),
        P(),
        P("ep", None),
        P("ep"),
    )
    out_specs = P("ep", "tp")
    return jax.shard_map(local, mesh=mesh, in_specs=in_specs, out_specs=out_specs, check_vma=False)
```

profile of v0, /device:TPU:0, one launch (start us, length us, event | category | flops | bytes accessed | tf_op | source)
XLA Modules:
  0.0 238.2 jit_solution(8258291260687447549)
XLA Ops:
  6.5 9.0 %all_gather.3 = bf16[128,2048]{1,0:T(8,128)(2,1)S(1)} all-gather(bf16[128,512]{1,0:T(8,128)(2,1)} %param.10), channel_id=1, replica_groups=mesh['ep'=8,'tp'=4] {'tp'}, dimensions={1}, use_global_device_ids=true | all-gather | bytes 655360 | tf_op jit(solution)/shard_map/all_gather | solution.py:61
  15.7 0.9 fusion.10
  16.6 0.8 copy-done.1
  18.1 1.1 broadcast_in_dim.58
  19.2 2.2 reshape.86
  21.4 3.7 %scatter_custom_fusion = bf16[384,2048]{1,0:T(8,128)(2,1)} fusion(s32[192]{0:T(256)S(1)} %bitcast.43, bf16[192,2048]{1,0:T(8,128)(2,1)} %reshape.86, bf16[]{:T(256)} %constant.10.clone.1), kind=kCustom, calls=%fused_computation.14 | custom fusion | bytes 1573376 | tf_op jit(solution)/shard_map/scatter | solution.py:77
  25.1 3.6 %reshape.69 = bf16[8,4,12,2048]{3,2,1,0:T(8,128)(2,1)} reshape(bf16[384,2048]{1,0:T(8,128)(2,1)} %scatter_custom_fusion) | data formatting | bytes 3145728 | tf_op jit(solution)/shard_map/reshape | solution.py:78
  28.7 2.8 %copy.29 = bf16[8,4,12,2048]{3,1,2,0:T(4,128)(2,1)S(1)} copy(bf16[8,4,12,2048]{3,2,1,0:T(8,128)(2,1)} %reshape.69) | data formatting | bytes 3145728 | tf_op jit(solution)/shard_map/reshape | solution.py:78
  31.5 43.1 %all_to_all.20 = bf16[8,4,12,2048]{3,1,2,0:T(4,128)(2,1)S(1)} all-to-all(bf16[8,4,12,2048]{3,1,2,0:T(4,128)(2,1)S(1)} %copy.29), channel_id=1, replica_groups=mesh['ep'=8,'tp'=4] {'ep'}, dimensions={0} | all-to-all | bytes 3145728 | tf_op jit(solution)/shard_map/all_to_all | solution.py:80
  74.6 0.9 copy.30
  75.5 22.5 %all_to_all.21 = bf16[8,4,12,2048]{3,0,2,1:T(8,128)(2,1)S(1)} all-to-all(bf16[8,4,12,2048]{3,0,2,1:T(8,128)(2,1)S(1)} %copy.30), channel_id=1, replica_groups=mesh['ep'=8,'tp'=4] {'tp'}, dimensions={1} | all-to-all | bytes 3145728 | tf_op jit(solution)/shard_map/all_to_all | solution.py:79
  98.0 2.2 copy.31
  100.3 3.6 %reshape.91 = bf16[384,2048,1]{1,0,2:T(8,128)(2,1)} reshape(bf16[8,4,12,2048]{3,2,1,0:T(8,128)(2,1)} %copy.31) | data formatting | bytes 3145728 | tf_op jit(solution)/shard_map/reshape | solution.py:29
  103.9 5.6 %fusion = f32[384,2,704]{0,2,1:T(8,128)S(1)} fusion(bf16[384,2048,1]{1,0,2:T(8,128)(2,1)} %reshape.91, bf16[1,2048,2,704]{1,3,2,0:T(8,128)(2,1)} %param.15), kind=kOutput, calls=%fused_computation.2 | convolution fusion | flops 2214592512 | bytes 9502720 | tf_op jit(solution)/shard_map/rd,dgf->rgf/dot_general | solution.py:30
  109.5 2.6 %fusion.4 = bf16[384,2048]{1,0:T(8,128)(2,1)} fusion(bf16[1,704,2048]{2,1,0:T(8,128)(2,1)S(1)} %copy-done, f32[384,2,704]{0,2,1:T(8,128)S(1)} %fusion), kind=kOutput, calls=%fused_computation.6 | convolution fusion | flops 1109704704 | bytes 6619136 | tf_op jit(solution)/shard_map/dot_general | solution.py:34
  112.2 3.6 %reshape.71 = bf16[8,4,12,2048]{3,2,1,0:T(8,128)(2,1)} reshape(bf16[384,2048]{1,0:T(8,128)(2,1)} %fusion.4) | data formatting | bytes 3145728 | tf_op jit(solution)/shard_map/reshape | solution.py:37
  115.8 4.0 %copy.32 = bf16[8,4,12,2048]{3,1,2,0:T(4,128)(2,1)} copy(bf16[8,4,12,2048]{3,2,1,0:T(8,128)(2,1)} %reshape.71) | data formatting | bytes 3145728 | tf_op jit(solution)/shard_map/reshape | solution.py:37
  119.7 4.6 %all-to-all-start.2 = ((bf16[8,4,12,2048]{3,1,2,0:T(4,128)(2,1)}), bf16[8,4,12,2048]{3,1,2,0:T(4,128)(2,1)}, u32[]{:S(2)}, u32[]{:S(2)}) async-start(bf16[8,4,12,2048]{3,1,2,0:T(4,128)(2,1)} %copy.32), calls=%async_computation.2 | async-start | bytes 3145728 | tf_op jit(solution)/shard_map/all_to_all | solution.py:88
  124.5 36.6 %all-to-all-done.2 = bf16[8,4,12,2048]{3,1,2,0:T(4,128)(2,1)} async-done(((bf16[8,4,12,2048]{3,1,2,0:T(4,128)(2,1)}), bf16[8,4,12,2048]{3,1,2,0:T(4,128)(2,1)}, u32[]{:S(2)}, u32[]{:S(2)}) %all-to-all-start.2) | async-done | bytes 1572896 | tf_op jit(solution)/shard_map/all_to_all | solution.py:88
  161.1 3.4 %copy.33 = bf16[8,4,12,2048]{3,0,2,1:T(8,128)(2,1)} copy(bf16[8,4,12,2048]{3,1,2,0:T(4,128)(2,1)} %all-to-all-done.2) | data formatting | bytes 3145728 | tf_op jit(solution)/shard_map/all_to_all | solution.py:88
  164.5 4.5 %all-to-all-start.3 = ((bf16[8,4,12,2048]{3,0,2,1:T(8,128)(2,1)}), bf16[8,4,12,2048]{3,0,2,1:T(8,128)(2,1)}, u32[]{:S(2)}, u32[]{:S(2)}) async-start(bf16[8,4,12,2048]{3,0,2,1:T(8,128)(2,1)} %copy.33), calls=%async_computation.3 | async-start | bytes 3145728 | tf_op jit(solution)/shard_map/all_to_all | solution.py:87
  169.5 2.8 %fusion.15 = f32[128,2,352]{0,2,1:T(8,128)S(1)} fusion(bf16[2048,2,352]{0,2,1:T(8,128)(2,1)} %param.13, bf16[128,2048]{1,0:T(8,128)(2,1)S(1)} %copy-done.2), kind=kOutput, calls=%fused_computation.17 | convolution fusion | flops 369098752 | bytes 3768320 | tf_op jit(solution)/shard_map/td,dgf->tgf/dot_general | solution.py:65
  172.4 1.5 fusion.21
  173.9 15.2 %all-to-all-done.3 = bf16[8,4,12,2048]{3,0,2,1:T(8,128)(2,1)} async-done(((bf16[8,4,12,2048]{3,0,2,1:T(8,128)(2,1)}), bf16[8,4,12,2048]{3,0,2,1:T(8,128)(2,1)}, u32[]{:S(2)}, u32[]{:S(2)}) %all-to-all-start.3) | async-done | bytes 1572896 | tf_op jit(solution)/shard_map/all_to_all | solution.py:87
  189.1 3.6 %copy.34 = bf16[8,4,12,2048]{3,2,1,0:T(8,128)(2,1)} copy(bf16[8,4,12,2048]{3,0,2,1:T(8,128)(2,1)} %all-to-all-done.3) | data formatting | bytes 3145728 | tf_op jit(solution)/shard_map/all_to_all | solution.py:87
  192.8 3.6 %reshape.72 = bf16[384,2048]{1,0:T(8,128)(2,1)} reshape(bf16[8,4,12,2048]{3,2,1,0:T(8,128)(2,1)} %copy.34) | data formatting | bytes 3145728 | tf_op jit(solution)/shard_map/reshape | solution.py:94
  196.4 4.4 %gather_fusion = bf16[192,2048]{1,0:T(8,128)(2,1)} fusion(bf16[384,2048]{1,0:T(8,128)(2,1)} %reshape.72, s32[1024]{0:T(1024)S(1)} %pad_clamp_fusion), kind=kCustom, calls=%fused_computation | custom fusion | bytes 1573632 | tf_op jit(solution)/shard_map/gather | solution.py:94
  200.8 2.2 reshape.73
  203.0 1.7 fusion.29
  204.7 1.7 fusion.17
  207.1 22.5 %reduce-scatter.2.cloned.1.call-done = f32[128,512]{1,0:T(8,128)} async-done(((f32[128,2048]{1,0:T(8,128)}), f32[128,512]{1,0:T(8,128)}) %reduce-scatter.2.cloned.1.call-update) | async-done | bytes 262160 | tf_op jit(solution)/shard_map/reduce_scatter | solution.py:98
  229.6 1.7 select_convert_fusion
  (36 shorter events, 1.5 us)
Async XLA Ops:
  6.5 103.0 %copy-start = (bf16[1,704,2048]{2,1,0:T(8,128)(2,1)S(1)}, bf16[1,704,2048]{2,1,0:T(8,128)(2,1)}, u32[]{:S(2)}) copy-start(bf16[1,704,2048]{2,1,0:T(8,128)(2,1)} %param.16) | copy-start | bytes 8650756
  6.5 10.9 %copy-start.6 = (s32[128,6]{0,1:T(8,128)S(1)}, s32[128,6]{0,1:T(8,128)}, u32[]{:S(2)}) copy-start(s32[128,6]{0,1:T(8,128)} %param.18) | copy-start | bytes 9220
  16.6 0.8 copy-start.1
  119.7 4.6 %copy-start.5 = (bf16[2048,8]{0,1:T(8,128)(2,1)S(1)}, bf16[2048,8]{0,1:T(8,128)(2,1)}, u32[]{:S(2)}) copy-start(bf16[2048,8]{0,1:T(8,128)(2,1)} %param.12) | copy-start | bytes 98308
  119.7 41.3 %all-to-all-start.2 = ((bf16[8,4,12,2048]{3,1,2,0:T(4,128)(2,1)}), bf16[8,4,12,2048]{3,1,2,0:T(4,128)(2,1)}, u32[]{:S(2)}, u32[]{:S(2)}) async-start(bf16[8,4,12,2048]{3,1,2,0:T(4,128)(2,1)} %copy.32), calls=%async_computation.2 | async-start | bytes 3145728 | tf_op jit(solution)/shard_map/all_to_all | solution.py:88
  164.5 4.5 %copy-start.7 = (s32[32]{0:T(128)S(1)}, s32[32]{0:T(128)}, u32[]{:S(2)}) copy-start(s32[32]{0:T(128)} %param.17) | copy-start | bytes 388
  164.5 5.0 %copy-start.2 = (bf16[128,2048]{1,0:T(8,128)(2,1)S(1)}, bf16[128,2048]{1,0:T(8,128)(2,1)}, u32[]{:S(2)}) copy-start(bf16[128,2048]{1,0:T(8,128)(2,1)} %copy-done.1) | copy-start | bytes 1572868
  164.5 24.6 %all-to-all-start.3 = ((bf16[8,4,12,2048]{3,0,2,1:T(8,128)(2,1)}), bf16[8,4,12,2048]{3,0,2,1:T(8,128)(2,1)}, u32[]{:S(2)}, u32[]{:S(2)}) async-start(bf16[8,4,12,2048]{3,0,2,1:T(8,128)(2,1)} %copy.33), calls=%async_computation.3 | async-start | bytes 3145728 | tf_op jit(solution)/shard_map/all_to_all | solution.py:87
  169.0 60.6 %reduce-scatter.2.cloned.1.call-start = ((), (), s32[]{:S(2)}) async-start(), calls=%async_computation.5 | async-start | bytes 1310720 | tf_op jit(solution)/shard_map/reduce_scatter | solution.py:98
  169.5 2.9 %copy-start.3 = (bf16[352,2048]{1,0:T(8,128)(2,1)S(1)}, bf16[352,2048]{1,0:T(8,128)(2,1)}, u32[]{:S(2)}) copy-start(bf16[352,2048]{1,0:T(8,128)(2,1)} %param.14) | copy-start | bytes 4325380
  203.0 26.6 %copy-start.4 = (bf16[128,512]{1,0:T(8,128)(2,1)S(1)}, bf16[128,512]{1,0:T(8,128)(2,1)}, u32[]{:S(2)}) copy-start(bf16[128,512]{1,0:T(8,128)(2,1)} %param.10) | copy-start | bytes 393220
Sparse Core Ops, SparseCore 0:
  206.6 22.9 reduce-scatter.1
where the time goes:
time: 239 us; the launch traced here: 238 us
  blocking collectives  74.6 us (31%)
  waiting for transfers between devices  74.3 us (31%)
  local copies, waits for them, and re-layouts  46.3 us (19%)
  matrix products  14.5 us (6%)
  between operations  14.2 us (6%)
  starting transfers between devices  9.12 us (4%)
  other arithmetic  5.13 us (2%)
    all_to_all x1, blocking collectives, local(): lax.all_to_all(outgoing, 'ep', split_axis=0, concat_axis=0, tiled=True)  43.1 us
    all_to_all x1, waiting for transfers between devices, local(): lax.all_to_all(computed, 'ep', split_axis=0, concat_axis=0, tiled=True)  36.6 us
    all_to_all x1, blocking collectives, local(): lax.all_to_all(lax.all_to_all(outgoing, 'ep', split_axis=0, concat_axis=0...  22.5 us
    reduce_scatter x1, waiting for transfers between devices, local(): lax.psum_scatter(partial_value, 'tp', scatter_dimension=1, tiled=True)  22.5 us
    all_to_all x1, waiting for transfers between devices, local(): lax.all_to_all(lax.all_to_all(computed, 'ep', split_axis=0, concat_axis=0...  15.2 us
    all_gather x1, blocking collectives, local(): full_rows = lax.all_gather(hidden_in, 'tp', axis=1, tiled=True)  8.98 us
    reshape x2, local copies, waits for them, and re-layouts, expert_apply(): return result.reshape(shape_in)  7.55 us
    reshape x2, local copies, waits for them, and re-layouts, local(): outgoing = outgoing.reshape(ep_count, tp_count, capacity, feature_width)  6.42 us
  transfers between devices with their start and end apart: 3, of which 3 were waited for; matrix products, arithmetic and copies ran while one was open for 2% of the time, Pallas kernels for 0%

commit v1 on v0

--- a/solution.py
+++ b/solution.py
@@ -2,6 +2,29 @@
 import jax.numpy as jnp
 from jax import lax
 from jax.sharding import PartitionSpec as P
+
+
+def split_up(x, dim, size):
+    lengths = x.shape
+    blocks = x.reshape(*lengths[:dim], size, lengths[dim] // size, *lengths[dim + 1 :])
+    return jnp.moveaxis(blocks, dim, 0)
+
+
+def laid_out(pieces, dim):
+    pieces = jnp.moveaxis(pieces, 0, dim)
+    lengths = pieces.shape
+    return pieces.reshape(*lengths[:dim], lengths[dim] * lengths[dim + 1], *lengths[dim + 2 :])
+
+
+def exchange_in_pairs(shard, axis, split_dim, concat_dim):
+    devices, here = (lax.axis_size(axis), lax.axis_index(axis))
+    parts = split_up(shard, split_dim, devices)
+    finished = [parts[here]]
+    for step in range(1, devices):
+        sent = parts[here ^ step]
+        finished.append(lax.ppermute(sent, axis, [(i, i ^ step) for i in range(devices)]))
+    parts = jnp.stack(finished)[here ^ jnp.arange(devices)]
+    return laid_out(parts, concat_dim)
 
 
 def gate_weights(normed_rows, choices, router_weight, slot_expert):
@@ -77,11 +100,7 @@
     outgoing = outgoing.at[placed].set(jnp.repeat(own_rows, top_count, axis=0))
     outgoing = outgoing.reshape(ep_count, tp_count, capacity, feature_width)
     arrived = lax.all_to_all(
-        lax.all_to_all(outgoing, "ep", split_axis=0, concat_axis=0, tiled=True),
-        "tp",
-        split_axis=1,
-        concat_axis=1,
-        tiled=True,
+        exchange_in_pairs(outgoing, "ep", 0, 0), "tp", split_axis=1, concat_axis=1, tiled=True
     )
     computed = expert_apply(arrived, slot_gate_up, slot_down)
     returned = lax.all_to_all(

time: 239 us -> 253 us (1.059)
  blocking collectives: 74.6 us -> 31.4 us
  waiting for transfers between devices: 74.3 us -> 101 us
  starting transfers between devices: 9.12 us -> 28.7 us
  local copies, waits for them, and re-layouts: 46.3 us -> 55.5 us
    all_to_all x2 -> x1, blocking collectives: 65.6 us -> 22.5 us  [local(): lax.all_to_all(exchange_in_pairs(outgoing, 'ep', 0, 0), 'tp', split_axis=...]
    ppermute x0 -> x7, waiting for transfers between devices: none -> 27.8 us  [exchange_in_pairs(): lax.ppermute(sent, axis, [(i, i ^ step) for i in range(devices)])]
    ppermute x0 -> x7, starting transfers between devices: none -> 11.9 us  [exchange_in_pairs(): lax.ppermute(sent, axis, [(i, i ^ step) for i in range(devices)])]
    all_to_all x1, starting transfers between devices: 4.6 us -> 12.3 us  [local(): lax.all_to_all(computed, 'ep', split_axis=0, concat_axis=0, tiled=True)]
    reshape x2 -> x0, local copies, waits for them, and re-layouts: 6.42 us -> none  [local(): outgoing = outgoing.reshape(ep_count, tp_count, capacity, feature_width)]
    gather x0 -> x2, local copies, waits for them, and re-layouts: none -> 6.08 us  [exchange_in_pairs(): parts = jnp.stack(finished)[here ^ jnp.arange(devices)]]
    another operation x0 -> x2, local copies, waits for them, and re-layouts: none -> 4.33 us  [the longest x1 3.6 us: split_up(): x.reshape(*lengths[:dim], size, lengths[dim] // size, *lengths[dim + 1:])]
    unnamed x16 -> x14, local copies, waits for them, and re-layouts: 0.81 us -> 4.37 us
  transfers between devices with their start and end apart: 3 -> 10, of which waited for: 3 -> 7; matrix products, arithmetic and copies ran while one was open for 2% -> 4% of each run, Pallas kernels for 0% -> 0%
where the time goes in v1:
time: 253 us; the launch traced here: 252 us
  waiting for transfers between devices  101 us (40%)
  local copies, waits for them, and re-layouts  55.5 us (22%)
  blocking collectives  31.4 us (12%)
  starting transfers between devices  28.7 us (11%)
  matrix products  15.2 us (6%)
  between operations  14.2 us (6%)
  other arithmetic  5.98 us (2%)
    all_to_all x1, waiting for transfers between devices, local(): lax.all_to_all(computed, 'ep', split_axis=0, concat_axis=0, tiled=True)  36.9 us
    ppermute x7, waiting for transfers between devices, exchange_in_pairs(): lax.ppermute(sent, axis, [(i, i ^ step) for i in range(devices)])  27.8 us
    all_to_all x1, blocking collectives, local(): lax.all_to_all(exchange_in_pairs(outgoing, 'ep', 0, 0), 'tp', split_axis=...  22.5 us
    reduce_scatter x1, waiting for transfers between devices, local(): lax.psum_scatter(partial_value, 'tp', scatter_dimension=1, tiled=True)  21.5 us
    all_to_all x1, waiting for transfers between devices, local(): lax.all_to_all(lax.all_to_all(computed, 'ep', split_axis=0, concat_axis=0...  15.3 us
    all_to_all x1, starting transfers between devices, local(): lax.all_to_all(computed, 'ep', split_axis=0, concat_axis=0, tiled=True)  12.3 us
    ppermute x7, starting transfers between devices, exchange_in_pairs(): lax.ppermute(sent, axis, [(i, i ^ step) for i in range(devices)])  11.9 us
    all_gather x1, blocking collectives, local(): full_rows = lax.all_gather(hidden_in, 'tp', axis=1, tiled=True)  8.86 us
  transfers between devices with their start and end apart: 10, of which 7 were waited for; matrix products, arithmetic and copies ran while one was open for 4% of the time, Pallas kernels for 0%

profile of v1, /device:TPU:0, one launch (start us, length us, event | category | flops | bytes accessed | tf_op | source)
XLA Modules:
  0.0 252.3 jit_solution(1723008322980112782)
XLA Ops:
  8.0 8.9 %all_gather.3 = bf16[128,2048]{1,0:T(8,128)(2,1)S(1)} all-gather(bf16[128,512]{1,0:T(8,128)(2,1)} %param.10), channel_id=1, replica_groups=mesh['ep'=8,'tp'=4] {'tp'}, dimensions={1}, use_global_device_ids=true | all-gather | bytes 655360 | tf_op jit(solution)/shard_map/all_gather | solution.py:84
  19.2 2.2 reshape.112
  21.3 3.7 %scatter_custom_fusion = bf16[384,2048]{1,0:T(8,128)(2,1)} fusion(s32[192]{0:T(256)S(1)} %bitcast.74, bf16[192,2048]{1,0:T(8,128)(2,1)} %reshape.112, bf16[]{:T(256)} %constant.11.clone.1), kind=kCustom, calls=%fused_computation.15 | custom fusion | bytes 1573376 | tf_op jit(solution)/shard_map/scatter | solution.py:100
  25.0 3.6 %reshape_reshape.3 = bf16[8,1,4,12,2048]{4,3,2,0,1:T(8,128)(2,1)} reshape(bf16[384,2048]{1,0:T(8,128)(2,1)} %scatter_custom_fusion) | data formatting | bytes 3145728 | tf_op jit(solution)/shard_map/reshape;reshape | solution.py:9
  28.6 2.4 dynamic-slice_bitcast_fusion
  34.5 2.6 %collective-permute-start.3 = (bf16[1,4,12,2048]{3,2,1,0:T(8,128)(2,1)S(1)}, bf16[1,4,12,2048]{3,2,1,0:T(8,128)(2,1)S(1)}, u32[]{:S(2)}, u32[]{:S(2)}) collective-permute-start(bf16[1,4,12,2048]{3,2,1,0:T(8,128)(2,1)S(1)} %get-tuple-element.10), channel_id=1, source_target_pairs={{0,16},{4,20},{8,24},{12,28},{16,0},{20,4},{24,8},{28,12},{1,17},{... | collective-permute-start | bytes 589832 | tf_op jit(solution)/shard_map/ppermute | solution.py:25
  39.6 3.6 %collective-permute-start.5 = (bf16[1,4,12,2048]{3,2,1,0:T(8,128)(2,1)S(1)}, bf16[1,4,12,2048]{3,2,1,0:T(8,128)(2,1)S(1)}, u32[]{:S(2)}, u32[]{:S(2)}) collective-permute-start(bf16[1,4,12,2048]{3,2,1,0:T(8,128)(2,1)S(1)} %get-tuple-element.8), channel_id=1, source_target_pairs={{0,24},{4,28},{8,16},{12,20},{16,8},{20,12},{24,0},{28,4},{1,25},{... | collective-permute-start | bytes 589832 | tf_op jit(solution)/shard_map/ppermute | solution.py:25
  43.9 8.1 %collective-permute-done.1 = bf16[1,4,12,2048]{3,2,1,0:T(8,128)(2,1)S(1)} collective-permute-done((bf16[1,4,12,2048]{3,2,1,0:T(8,128)(2,1)S(1)}, bf16[1,4,12,2048]{3,2,1,0:T(8,128)(2,1)S(1)}, u32[]{:S(2)}, u32[]{:S(2)}) %collective-permute-start.1) | collective-permute-done | bytes 196640 | tf_op jit(solution)/shard_map/ppermute | solution.py:25
  53.7 2.5 %collective-permute-done.2 = bf16[1,4,12,2048]{3,2,1,0:T(8,128)(2,1)S(1)} collective-permute-done((bf16[1,4,12,2048]{3,2,1,0:T(8,128)(2,1)S(1)}, bf16[1,4,12,2048]{3,2,1,0:T(8,128)(2,1)S(1)}, u32[]{:S(2)}, u32[]{:S(2)}) %collective-permute-start.2) | collective-permute-done | bytes 196640 | tf_op jit(solution)/shard_map/ppermute | solution.py:25
  57.7 15.9 %collective-permute-done.4 = bf16[1,4,12,2048]{3,2,1,0:T(8,128)(2,1)S(1)} collective-permute-done((bf16[1,4,12,2048]{3,2,1,0:T(8,128)(2,1)S(1)}, bf16[1,4,12,2048]{3,2,1,0:T(8,128)(2,1)S(1)}, u32[]{:S(2)}, u32[]{:S(2)}) %collective-permute-start.4) | collective-permute-done | bytes 196640 | tf_op jit(solution)/shard_map/ppermute | solution.py:25
  75.8 3.6 %gather_fusion = bf16[8,4,12,2048]{3,2,1,0:T(8,128)(2,1)} fusion(bf16[8,4,12,2048]{3,2,1,0:T(8,128)(2,1)} %bitcast.21, s32[1024]{0:T(1024)S(1)} %pad_clamp_fusion.1), kind=kCustom, calls=%fused_computation | custom fusion | bytes 3145760 | tf_op jit(solution)/shard_map/gather | solution.py:26
  79.5 2.5 copy.28
  81.9 22.5 %all_to_all.15 = bf16[8,4,12,2048]{3,0,2,1:T(8,128)(2,1)S(1)} all-to-all(bf16[8,4,12,2048]{3,0,2,1:T(8,128)(2,1)S(1)} %copy.28), channel_id=1, replica_groups=mesh['ep'=8,'tp'=4] {'tp'}, dimensions={1} | all-to-all | bytes 3145728 | tf_op jit(solution)/shard_map/all_to_all | solution.py:102
  104.4 2.2 copy.29
  106.7 3.6 %reshape.118 = bf16[384,2048,1]{1,0,2:T(8,128)(2,1)} reshape(bf16[8,4,12,2048]{3,2,1,0:T(8,128)(2,1)} %copy.29) | data formatting | bytes 3145728 | tf_op jit(solution)/shard_map/reshape | solution.py:52
  110.3 5.6 %fusion = f32[384,2,704]{0,2,1:T(8,128)S(1)} fusion(bf16[384,2048,1]{1,0,2:T(8,128)(2,1)} %reshape.118, bf16[1,2048,2,704]{1,3,2,0:T(8,128)(2,1)} %param.15), kind=kOutput, calls=%fused_computation.3 | convolution fusion | flops 2214592512 | bytes 9502720 | tf_op jit(solution)/shard_map/rd,dgf->rgf/dot_general | solution.py:53
  116.0 2.7 %fusion.4 = bf16[384,2048]{1,0:T(8,128)(2,1)} fusion(bf16[1,704,2048]{2,1,0:T(8,128)(2,1)S(1)} %copy-done, f32[384,2,704]{0,2,1:T(8,128)S(1)} %fusion), kind=kOutput, calls=%fused_computation.7 | convolution fusion | flops 1109704704 | bytes 6619136 | tf_op jit(solution)/shard_map/dot_general | solution.py:57
  118.6 3.6 %reshape.87 = bf16[8,4,12,2048]{3,2,1,0:T(8,128)(2,1)} reshape(bf16[384,2048]{1,0:T(8,128)(2,1)} %fusion.4) | data formatting | bytes 3145728 | tf_op jit(solution)/shard_map/reshape | solution.py:60
  122.2 4.0 %copy.30 = bf16[8,4,12,2048]{3,1,2,0:T(4,128)(2,1)} copy(bf16[8,4,12,2048]{3,2,1,0:T(8,128)(2,1)} %reshape.87) | data formatting | bytes 3145728 | tf_op jit(solution)/shard_map/reshape | solution.py:60
  126.2 12.3 %all-to-all-start.1 = ((bf16[8,4,12,2048]{3,1,2,0:T(4,128)(2,1)}), bf16[8,4,12,2048]{3,1,2,0:T(4,128)(2,1)}, u32[]{:S(2)}, u32[]{:S(2)}) async-start(bf16[8,4,12,2048]{3,1,2,0:T(4,128)(2,1)} %copy.30), calls=%async_computation.1 | async-start | bytes 3145728 | tf_op jit(solution)/shard_map/all_to_all | solution.py:107
  139.4 36.9 %all-to-all-done.1 = bf16[8,4,12,2048]{3,1,2,0:T(4,128)(2,1)} async-done(((bf16[8,4,12,2048]{3,1,2,0:T(4,128)(2,1)}), bf16[8,4,12,2048]{3,1,2,0:T(4,128)(2,1)}, u32[]{:S(2)}, u32[]{:S(2)}) %all-to-all-start.1) | async-done | bytes 1572896 | tf_op jit(solution)/shard_map/all_to_all | solution.py:107
  176.2 3.4 %copy.31 = bf16[8,4,12,2048]{3,0,2,1:T(8,128)(2,1)} copy(bf16[8,4,12,2048]{3,1,2,0:T(4,128)(2,1)} %all-to-all-done.1) | data formatting | bytes 3145728 | tf_op jit(solution)/shard_map/all_to_all | solution.py:107
  179.7 4.5 %all-to-all-start.2 = ((bf16[8,4,12,2048]{3,0,2,1:T(8,128)(2,1)}), bf16[8,4,12,2048]{3,0,2,1:T(8,128)(2,1)}, u32[]{:S(2)}, u32[]{:S(2)}) async-start(bf16[8,4,12,2048]{3,0,2,1:T(8,128)(2,1)} %copy.31), calls=%async_computation.2 | async-start | bytes 3145728 | tf_op jit(solution)/shard_map/all_to_all | solution.py:106
  184.7 2.8 %fusion.15 = f32[128,2,352]{0,2,1:T(8,128)S(1)} fusion(bf16[2048,2,352]{0,2,1:T(8,128)(2,1)} %param.13, bf16[128,2048]{1,0:T(8,128)(2,1)S(1)} %fusion.10), kind=kOutput, calls=%fused_computation.18 | convolution fusion | flops 369098752 | bytes 3768320 | tf_op jit(solution)/shard_map/td,dgf->tgf/dot_general | solution.py:88
  189.0 15.3 %all-to-all-done.2 = bf16[8,4,12,2048]{3,0,2,1:T(8,128)(2,1)} async-done(((bf16[8,4,12,2048]{3,0,2,1:T(8,128)(2,1)}), bf16[8,4,12,2048]{3,0,2,1:T(8,128)(2,1)}, u32[]{:S(2)}, u32[]{:S(2)}) %all-to-all-start.2) | async-done | bytes 1572896 | tf_op jit(solution)/shard_map/all_to_all | solution.py:106
  204.3 3.7 %copy.32 = bf16[8,4,12,2048]{3,2,1,0:T(8,128)(2,1)} copy(bf16[8,4,12,2048]{3,0,2,1:T(8,128)(2,1)} %all-to-all-done.2) | data formatting | bytes 3145728 | tf_op jit(solution)/shard_map/all_to_all | solution.py:106
  208.0 3.6 %reshape.88 = bf16[384,2048]{1,0:T(8,128)(2,1)} reshape(bf16[8,4,12,2048]{3,2,1,0:T(8,128)(2,1)} %copy.32) | data formatting | bytes 3145728 | tf_op jit(solution)/shard_map/reshape | solution.py:113
  211.6 4.4 %gather_fusion.1 = bf16[192,2048]{1,0:T(8,128)(2,1)} fusion(bf16[384,2048]{1,0:T(8,128)(2,1)} %reshape.88, s32[1024]{0:T(1024)S(1)} %pad_clamp_fusion), kind=kCustom, calls=%fused_computation.1 | custom fusion | bytes 1573632 | tf_op jit(solution)/shard_map/gather | solution.py:113
  216.0 2.2 reshape.89
  219.9 1.7 fusion.17
  222.3 21.5 %reduce-scatter.2.cloned.1.call-done = f32[128,512]{1,0:T(8,128)} async-done(((f32[128,2048]{1,0:T(8,128)}), f32[128,512]{1,0:T(8,128)}) %reduce-scatter.2.cloned.1.call-update) | async-done | bytes 262160 | tf_op jit(solution)/shard_map/reduce_scatter | solution.py:117
  243.8 1.7 select_convert_fusion
  (51 shorter events, 20.3 us)
Async XLA Ops:
  6.5 109.4 %copy-start = (bf16[1,704,2048]{2,1,0:T(8,128)(2,1)S(1)}, bf16[1,704,2048]{2,1,0:T(8,128)(2,1)}, u32[]{:S(2)}) copy-start(bf16[1,704,2048]{2,1,0:T(8,128)(2,1)} %param.16) | copy-start | bytes 8650756
  31.0 8.6 %collective-permute-start = (bf16[1,4,12,2048]{3,2,1,0:T(8,128)(2,1)S(1)}, bf16[1,4,12,2048]{3,2,1,0:T(8,128)(2,1)S(1)}, u32[]{:S(2)}, u32[]{:S(2)}) collective-permute-start(bf16[1,4,12,2048]{3,2,1,0:T(8,128)(2,1)S(1)} %get-tuple-element.13), channel_id=1, source_target_pairs={{0,4},{4,0},{8,12},{12,8},{16,20},{20,16},{24,28},{28,24},{1,5},{5... | collective-permute-start | bytes 589832 | tf_op jit(solution)/shard_map/ppermute | solution.py:25
  32.5 19.5 %collective-permute-start.1 = (bf16[1,4,12,2048]{3,2,1,0:T(8,128)(2,1)S(1)}, bf16[1,4,12,2048]{3,2,1,0:T(8,128)(2,1)S(1)}, u32[]{:S(2)}, u32[]{:S(2)}) collective-permute-start(bf16[1,4,12,2048]{3,2,1,0:T(8,128)(2,1)S(1)} %get-tuple-element.12), channel_id=1, source_target_pairs={{0,8},{4,12},{8,0},{12,4},{16,24},{20,28},{24,16},{28,20},{1,9},{5... | collective-permute-start | bytes 589832 | tf_op jit(solution)/shard_map/ppermute | solution.py:25
  34.1 22.2 %collective-permute-start.2 = (bf16[1,4,12,2048]{3,2,1,0:T(8,128)(2,1)S(1)}, bf16[1,4,12,2048]{3,2,1,0:T(8,128)(2,1)S(1)}, u32[]{:S(2)}, u32[]{:S(2)}) collective-permute-start(bf16[1,4,12,2048]{3,2,1,0:T(8,128)(2,1)S(1)} %get-tuple-element.11), channel_id=1, source_target_pairs={{0,12},{4,8},{8,4},{12,0},{16,28},{20,24},{24,20},{28,16},{1,13},{... | collective-permute-start | bytes 589832 | tf_op jit(solution)/shard_map/ppermute | solution.py:25
  34.5 22.5 %collective-permute-start.3 = (bf16[1,4,12,2048]{3,2,1,0:T(8,128)(2,1)S(1)}, bf16[1,4,12,2048]{3,2,1,0:T(8,128)(2,1)S(1)}, u32[]{:S(2)}, u32[]{:S(2)}) collective-permute-start(bf16[1,4,12,2048]{3,2,1,0:T(8,128)(2,1)S(1)} %get-tuple-element.10), channel_id=1, source_target_pairs={{0,16},{4,20},{8,24},{12,28},{16,0},{20,4},{24,8},{28,12},{1,17},{... | collective-permute-start | bytes 589832 | tf_op jit(solution)/shard_map/ppermute | solution.py:25
  37.1 36.6 %collective-permute-start.4 = (bf16[1,4,12,2048]{3,2,1,0:T(8,128)(2,1)S(1)}, bf16[1,4,12,2048]{3,2,1,0:T(8,128)(2,1)S(1)}, u32[]{:S(2)}, u32[]{:S(2)}) collective-permute-start(bf16[1,4,12,2048]{3,2,1,0:T(8,128)(2,1)S(1)} %get-tuple-element.9), channel_id=1, source_target_pairs={{0,20},{4,16},{8,28},{12,24},{16,4},{20,0},{24,12},{28,8},{1,21},{... | collective-permute-start | bytes 589832 | tf_op jit(solution)/shard_map/ppermute | solution.py:25
  39.6 34.8 %collective-permute-start.5 = (bf16[1,4,12,2048]{3,2,1,0:T(8,128)(2,1)S(1)}, bf16[1,4,12,2048]{3,2,1,0:T(8,128)(2,1)S(1)}, u32[]{:S(2)}, u32[]{:S(2)}) collective-permute-start(bf16[1,4,12,2048]{3,2,1,0:T(8,128)(2,1)S(1)} %get-tuple-element.8), channel_id=1, source_target_pairs={{0,24},{4,28},{8,16},{12,20},{16,8},{20,12},{24,0},{28,4},{1,25},{... | collective-permute-start | bytes 589832 | tf_op jit(solution)/shard_map/ppermute | solution.py:25
  52.0 23.1 %collective-permute-start.6 = (bf16[1,4,12,2048]{3,2,1,0:T(8,128)(2,1)S(1)}, bf16[1,4,12,2048]{3,2,1,0:T(8,128)(2,1)S(1)}, u32[]{:S(2)}, u32[]{:S(2)}) collective-permute-start(bf16[1,4,12,2048]{3,2,1,0:T(8,128)(2,1)S(1)} %get-tuple-element.7), channel_id=1, source_target_pairs={{0,28},{4,24},{8,20},{12,16},{16,12},{20,8},{24,4},{28,0},{1,29},{... | collective-permute-start | bytes 589832 | tf_op jit(solution)/shard_map/ppermute | solution.py:25
  126.2 50.1 %all-to-all-start.1 = ((bf16[8,4,12,2048]{3,1,2,0:T(4,128)(2,1)}), bf16[8,4,12,2048]{3,1,2,0:T(4,128)(2,1)}, u32[]{:S(2)}, u32[]{:S(2)}) async-start(bf16[8,4,12,2048]{3,1,2,0:T(4,128)(2,1)} %copy.30), calls=%async_computation.1 | async-start | bytes 3145728 | tf_op jit(solution)/shard_map/all_to_all | solution.py:107
  179.7 4.6 %copy-start.3 = (s32[32]{0:T(128)S(1)}, s32[32]{0:T(128)}, u32[]{:S(2)}) copy-start(s32[32]{0:T(128)} %param.17) | copy-start | bytes 388
  179.7 24.6 %all-to-all-start.2 = ((bf16[8,4,12,2048]{3,0,2,1:T(8,128)(2,1)}), bf16[8,4,12,2048]{3,0,2,1:T(8,128)(2,1)}, u32[]{:S(2)}, u32[]{:S(2)}) async-start(bf16[8,4,12,2048]{3,0,2,1:T(8,128)(2,1)} %copy.31), calls=%async_computation.2 | async-start | bytes 3145728 | tf_op jit(solution)/shard_map/all_to_all | solution.py:106
  184.2 59.6 %reduce-scatter.2.cloned.1.call-start = ((), (), s32[]{:S(2)}) async-start(), calls=%async_computation.4 | async-start | bytes 1310720 | tf_op jit(solution)/shard_map/reduce_scatter | solution.py:117
  184.7 2.9 %copy-start.1 = (bf16[352,2048]{1,0:T(8,128)(2,1)S(1)}, bf16[352,2048]{1,0:T(8,128)(2,1)}, u32[]{:S(2)}) copy-start(bf16[352,2048]{1,0:T(8,128)(2,1)} %param.14) | copy-start | bytes 4325380
  216.0 27.8 %copy-start.2 = (bf16[128,512]{1,0:T(8,128)(2,1)S(1)}, bf16[128,512]{1,0:T(8,128)(2,1)}, u32[]{:S(2)}) copy-start(bf16[128,512]{1,0:T(8,128)(2,1)} %param.10) | copy-start | bytes 393220
Sparse Core Ops, SparseCore 0:
  221.8 21.9 reduce-scatter.1
